TPU v7x, 512 devices: a whole 4x8x8 slice. The times are simulated.
512 devices in a mesh: hyp: 8 (over y), prow: 16 (over x, z_lo), pcol: 4 (over z_hi, core).
Axes of the slice: x: 4, y: 8, z: 8 (z_hi: 2, z_lo: 4; z = z_hi * 4 + z_lo), core: 2. Of those that a mesh axis runs over, the one named last changes fastest.
Arguments:
- sigma_rows: bfloat16 [8, 8192, 8192], P('hyp', 'prow', 'pcol'), may hold values from -1 to 1, as said below
- panel: bfloat16 [8, 8192, 2, 384], P('hyp', ('prow', 'pcol')), may hold values from -0.59765625 to 0.59765625
- live_block_rows: int32 [2, 64], P(None, ('prow', 'pcol')), may hold values from 1 to 128, 6144 in all within a row
- inv_diag: bfloat16 [8, 2, 384, 384], P('hyp', None, ('prow', 'pcol')), may hold values from -0.3125 to 0.3125
- quad_weight: float32 [8], P('hyp'), may hold values from 0.05 to 0.5
Outputs:
- sigma_panel: bfloat16 [8, 8192, 2, 384], P('hyp', ('prow', 'pcol'))
- marginal: float32 [2, 384, 384], replicated
Inputs may be any that keep to these rules, and one draw needn't show every extreme that they name: `sigma_rows`: each quadrature point's matrix is symmetric.
All inputs are finite; a program needn't handle non-finite values. No bound on the sum of `live_block_rows` on one device may be relied on, other than what follows from the above.
Results may differ from a plain program's by a relative error of at most 0.0004.
Values may be sent and summed in bfloat16 or wider, within the bound.
A program may use at most 64 MiB of HBM per device.

v0:
```python
import jax
import jax.numpy as jnp
from jax import lax
from jax.sharding import PartitionSpec as P


def cut_along(x, dim, length):
    shape = x.shape
    pieces = x.reshape(*shape[:dim], length, shape[dim] // length, *shape[dim + 1 :])
    return jnp.moveaxis(pieces, dim, 0)


def sent_and_summed(x, axis, dim):
    length = lax.axis_size(axis)
    pieces = lax.all_to_all(cut_along(x, dim, length), axis, 0, 0, tiled=True)
    return jnp.sum(pieces, axis=0)


def on_device(sigma_rows, panel, live_block_rows, inv_diag, quad_weight):
    height = panel.shape[1]
    width = panel.shape[3]
    supernode_list = panel.shape[2]
    offsets = lax.broadcasted_iota(jnp.int32, (height, supernode_list), 0)
    active = offsets < live_block_rows[:, 0][None, :]
    masked_panel = jnp.where(active[:, :, None], panel[0], jnp.zeros_like(panel[0]))
    grid_rows = lax.axis_size("prow")
    column = lax.axis_index("pcol")
    gathered = lax.all_gather(masked_panel, ("prow", "pcol"), axis=0, tiled=True)
    extent = height * grid_rows
    column_panel = lax.dynamic_slice_in_dim(gathered, column * extent, extent, 0)
    flattened = column_panel.reshape(column_panel.shape[0], supernode_list * width)
    covariance_block = sigma_rows[0]
    applied = sent_and_summed(
        jnp.dot(covariance_block, flattened, preferred_element_type=jnp.float32), "pcol", 0
    )
    applied_full = applied.reshape(height, supernode_list, width)
    half_applied_product = applied_full.astype(jnp.bfloat16)
    sigma_panel = jnp.where(
        active[:, :, None], -half_applied_product, jnp.zeros_like(half_applied_product)
    )[None]
    coupling_block = jnp.einsum(
        "vwg,vwe->wge",
        masked_panel.astype(jnp.float32),
        applied_full,
        precision=lax.Precision.HIGHEST,
    )
    inverse_local = inv_diag[0]
    diagonal = jnp.einsum(
        "skp,skq->spq", inverse_local, inverse_local, preferred_element_type=jnp.float32
    )
    partial_sum = coupling_block + diagonal
    marginal = lax.psum(quad_weight[0] * partial_sum, ("hyp", "prow", "pcol"))
    return (sigma_panel, marginal)


def solution(mesh):
    in_specs = (
        P("hyp", "prow", "pcol"),
        P("hyp", ("prow", "pcol"), None, None),
        P(None, ("prow", "pcol")),
        P("hyp", None, ("prow", "pcol"), None),
        P("hyp"),
    )
    out_specs = (P("hyp", ("prow", "pcol"), None, None), P())
    return jax.shard_map(
        on_device, mesh=mesh, in_specs=in_specs, out_specs=out_specs, check_vma=False
    )
```

profile of v0, /device:TPU:1, one launch (start us, length us, event | category | flops | bytes accessed | tf_op | source)
XLA Modules:
  0.0 488.1 jit_solution(7371981305845828398)
XLA Ops:
  7.2 0.0 copy-start
  7.2 0.0 all-gather.2.cloned.1.call-start
  7.2 0.8 iota_compare_fusion
  8.0 1.9 broadcast_select_fusion
  9.9 0.0 all-gather.2.cloned.1.call-update
  10.0 135.1 %all-gather.2.cloned.1.call-done = bf16[8192,2,384]{2,1,0:T(2,128)(2,1)} async-done(((bf16[128,2,384]{2,1,0:T(2,128)(2,1)}), bf16[8192,2,384]{2,1,0:T(2,128)(2,1)}) %all-gather.2.cloned.1.call-update) | async-done | bytes 12582928 | tf_op jit(solution)/shard_map/all_gather | solution.py:28
  145.1 4.7 constant_dynamic-slice_fusion
  149.8 0.6 copy.21
  150.4 2.9 fusion
  153.4 6.0 %all-to-all-start = ((f32[4,128,768]{2,1,0:T(8,128)}), f32[4,128,768]{2,1,0:T(8,128)}, u32[]{:S(2)}, u32[]{:S(2)}) async-start(f32[4,128,768]{2,1,0:T(8,128)} %bitcast.19), calls=%async_computation | async-start | bytes 3145728 | tf_op jit(solution)/shard_map/all_to_all | solution.py:15
  160.0 0.0 copy-done.2
  160.1 0.4 fusion.4
  160.4 0.0 copy-start.1
  160.4 29.1 %all-to-all-done = f32[4,128,768]{2,1,0:T(8,128)} async-done(((f32[4,128,768]{2,1,0:T(8,128)}), f32[4,128,768]{2,1,0:T(8,128)}, u32[]{:S(2)}, u32[]{:S(2)}) %all-to-all-start) | async-done | bytes 1572896 | tf_op jit(solution)/shard_map/all_to_all | solution.py:15
  189.5 2.3 reduce_sum.9
  191.8 1.9 copy.15
  193.7 0.0 copy-done.1
  193.7 2.7 fusion.2
  196.4 0.0 all-reduce.2.cloned.1.call-update
  196.4 1.0 convert_negate_fusion
  197.5 0.1 neg.14
  197.5 1.0 broadcast_select_fusion.1
  198.5 280.4 %all-reduce.2.cloned.1.call-done = f32[2,384,384]{2,1,0:T(8,128)} async-done(((f32[2,384,384]{2,1,0:T(8,128)}), f32[2,384,384]{2,1,0:T(8,128)}) %all-reduce.2.cloned.1.call-update) | async-done | bytes 1179664 | tf_op jit(solution)/shard_map/psum | solution.py:52
  478.9 2.4 copy.28
  (3 shorter events, 0.0 us)
Async XLA Ops:
  7.2 143.2 %copy-start = (bf16[1,512,2048]{2,1,0:T(8,128)(2,1)S(1)}, bf16[1,512,2048]{2,1,0:T(8,128)(2,1)}, u32[]{:S(2)}) copy-start(bf16[1,512,2048]{2,1,0:T(8,128)(2,1)} %param.5) | copy-start | bytes 6291460
  7.2 137.9 %all-gather.2.cloned.1.call-start = ((), (), s32[]{:S(2)}) async-start(), calls=%async_computation.1 | async-start | bytes 12779520 | tf_op jit(solution)/shard_map/all_gather | solution.py:28
  153.3 6.7 %copy-start.2 = (bf16[1,2,6,384]{3,1,2,0:T(2,128)(2,1)S(1)}, bf16[1,2,6,384]{3,1,2,0:T(2,128)(2,1)}, u32[]{:S(2)}) copy-start(bf16[1,2,6,384]{3,1,2,0:T(2,128)(2,1)} %param.8) | copy-start | bytes 27652
  153.4 36.2 %all-to-all-start = ((f32[4,128,768]{2,1,0:T(8,128)}), f32[4,128,768]{2,1,0:T(8,128)}, u32[]{:S(2)}, u32[]{:S(2)}) async-start(f32[4,128,768]{2,1,0:T(8,128)} %bitcast.19), calls=%async_computation | async-start | bytes 3145728 | tf_op jit(solution)/shard_map/all_to_all | solution.py:15
  159.4 319.5 %all-reduce.2.cloned.1.call-start = ((), (), s32[]{:S(2)}) async-start(), calls=%async_computation.2 | async-start | bytes 2359296 | tf_op jit(solution)/shard_map/psum | solution.py:52
  160.4 33.3 %copy-start.1 = (bf16[128,2,384]{2,1,0:T(2,128)(2,1)S(1)}, bf16[128,2,384]{2,1,0:T(2,128)(2,1)}, u32[]{:S(2)}) copy-start(bf16[128,2,384]{2,1,0:T(2,128)(2,1)} %broadcast_select_fusion) | copy-start | bytes 589828
Sparse Core Ops, SparseCore 0:
  10.7 134.2 all-gather.1
  196.6 282.2 all-reduce.1
where the time goes:
time: 489 us; the launch traced here: 488 us
  waiting for transfers between devices  445 us (91%)
  between operations  14.8 us (3%)
  local copies, waits for them, and re-layouts  9.67 us (2%)
  other arithmetic  6.99 us (1%)
  starting transfers between devices  6.08 us (1%)
  matrix products  6.01 us (1%)
    psum x1, waiting for transfers between devices, on_device(): marginal = lax.psum(quad_weight[0] * partial_sum, ('hyp', 'prow', 'pcol'))  280 us
    all_gather x1, waiting for transfers between devices, on_device(): lax.all_gather(masked_panel, ('prow', 'pcol'), axis=0, tiled=True)  135 us
    all_to_all x1, waiting for transfers between devices, sent_and_summed(): pieces = lax.all_to_all(cut_along(x, dim, length), axis, 0, 0, tiled=True)  29.1 us
  transfers between devices with their start and end apart: 3, of which 3 were waited for; matrix products, arithmetic and copies ran while one was open for 0% of the time, Pallas kernels for 0%

commit v1 on v0

--- a/solution.py
+++ b/solution.py
@@ -25,7 +25,12 @@
     masked_panel = jnp.where(active[:, :, None], panel[0], jnp.zeros_like(panel[0]))
     grid_rows = lax.axis_size("prow")
     column = lax.axis_index("pcol")
-    gathered = lax.all_gather(masked_panel, ("prow", "pcol"), axis=0, tiled=True)
+    gathered = jnp.concatenate(
+        lax.all_to_all(
+            jnp.stack([masked_panel] * lax.axis_size(("prow", "pcol"))), ("prow", "pcol"), 0, 0
+        ),
+        axis=0,
+    )
     extent = height * grid_rows
     column_panel = lax.dynamic_slice_in_dim(gathered, column * extent, extent, 0)
     flattened = column_panel.reshape(column_panel.shape[0], supernode_list * width)

time: 489 us -> 650 us (1.33)
  waiting for transfers between devices: 445 us -> 581 us
  starting transfers between devices: 6.08 us -> 23.6 us
  local copies, waits for them, and re-layouts: 9.67 us -> 17.8 us
    all_to_all x0 -> x1, waiting for transfers between devices: none -> 273 us  [on_device(): lax.all_to_all(jnp.stack([masked_panel] * lax.axis_size(('prow', 'pcol'))...]
    all_gather x1 -> x0, waiting for transfers between devices: 135 us -> none  [on_device(): lax.all_gather(masked_panel, ('prow', 'pcol'), axis=0, tiled=True)]
    all_to_all x0 -> x1, starting transfers between devices: none -> 15 us  [on_device(): lax.all_to_all(jnp.stack([masked_panel] * lax.axis_size(('prow', 'pcol'))...]
    another operation x0 -> x1, local copies, waits for them, and re-layouts: none -> 8.13 us  [on_device(): jnp.stack([masked_panel] * lax.axis_size(('prow', 'pcol')))]
where the time goes in v1:
time: 650 us
  waiting for transfers between devices  581 us (89%)
  starting transfers between devices  23.6 us (4%)
  local copies, waits for them, and re-layouts  17.8 us (3%)
  between operations  14.8 us (2%)
  other arithmetic  6.61 us (1%)
    psum x1, waiting for transfers between devices, on_device(): marginal = lax.psum(quad_weight[0] * partial_sum, ('hyp', 'prow', 'pcol'))  280 us
    all_to_all x1, waiting for transfers between devices, on_device(): lax.all_to_all(jnp.stack([masked_panel] * lax.axis_size(('prow', 'pcol'))...  273 us
    all_to_all x1, waiting for transfers between devices, sent_and_summed(): pieces = lax.all_to_all(cut_along(x, dim, length), axis, 0, 0, tiled=True)  28 us
    all_to_all x1, starting transfers between devices, on_device(): lax.all_to_all(jnp.stack([masked_panel] * lax.axis_size(('prow', 'pcol'))...  15 us
  transfers between devices with their start and end apart: 3, of which 3 were waited for; matrix products, arithmetic and copies ran while one was open for 0% of the time, Pallas kernels for 0%

profile of v1, /device:TPU:1, one launch (start us, length us, event | category | flops | bytes accessed | tf_op | source)
XLA Modules:
  0.0 649.7 jit_solution(7444574902736371328)
XLA Ops:
  7.2 0.0 copy-start
  7.2 0.8 iota_compare_fusion
  8.0 1.2 fusion.3
  9.2 8.1 %stack.5 = bf16[64,128,2,384]{3,2,1,0:T(2,128)(2,1)} broadcast(bf16[128,2,384]{2,1,0:T(2,128)(2,1)S(1)} %fusion.3), dimensions={1,2,3} | broadcast | bytes 12779520 | tf_op jit(solution)/shard_map/stack | solution.py:30
  17.4 15.0 %all-to-all-start = ((bf16[64,128,2,384]{3,2,1,0:T(2,128)(2,1)}), bf16[64,128,2,384]{3,2,1,0:T(2,128)(2,1)}, u32[]{:S(2)}, u32[]{:S(2)}) async-start(bf16[64,128,2,384]{3,2,1,0:T(2,128)(2,1)} %stack.5), calls=%async_computation | async-start | bytes 25165824 | tf_op jit(solution)/shard_map/all_to_all | solution.py:29
  32.4 272.8 %all-to-all-done = bf16[64,128,2,384]{3,2,1,0:T(2,128)(2,1)} async-done(((bf16[64,128,2,384]{3,2,1,0:T(2,128)(2,1)}), bf16[64,128,2,384]{3,2,1,0:T(2,128)(2,1)}, u32[]{:S(2)}, u32[]{:S(2)}) %all-to-all-start) | async-done | bytes 12582944 | tf_op jit(solution)/shard_map/all_to_all | solution.py:29
  305.1 4.7 constant_dynamic-slice_fusion
  309.8 0.6 copy.21
  310.5 2.9 fusion
  313.4 8.6 %all-to-all-start.1 = ((f32[4,128,768]{2,1,0:T(8,128)}), f32[4,128,768]{2,1,0:T(8,128)}, u32[]{:S(2)}, u32[]{:S(2)}) async-start(f32[4,128,768]{2,1,0:T(8,128)} %bitcast.22), calls=%async_computation.1 | async-start | bytes 3145728 | tf_op jit(solution)/shard_map/all_to_all | solution.py:15
  322.0 0.0 all-reduce.2.cloned.1.call-start
  322.7 0.3 broadcast_select_fusion
  323.0 0.0 copy-done.2
  323.0 0.4 fusion.5
  323.4 28.0 %all-to-all-done.1 = f32[4,128,768]{2,1,0:T(8,128)} async-done(((f32[4,128,768]{2,1,0:T(8,128)}), f32[4,128,768]{2,1,0:T(8,128)}, u32[]{:S(2)}, u32[]{:S(2)}) %all-to-all-start.1) | async-done | bytes 1572896 | tf_op jit(solution)/shard_map/all_to_all | solution.py:15
  351.4 2.3 reduce_sum.9
  353.7 1.9 copy.15
  355.6 2.7 fusion.2
  358.3 0.0 all-reduce.2.cloned.1.call-update
  358.3 1.0 convert_negate_fusion
  359.3 0.1 neg.14
  359.4 1.0 broadcast_select_fusion.1
  360.4 280.1 %all-reduce.2.cloned.1.call-done = f32[2,384,384]{2,1,0:T(8,128)} async-done(((f32[2,384,384]{2,1,0:T(8,128)}), f32[2,384,384]{2,1,0:T(8,128)}) %all-reduce.2.cloned.1.call-update) | async-done | bytes 1179664 | tf_op jit(solution)/shard_map/psum | solution.py:57
  640.5 2.4 copy.28
  (4 shorter events, 0.0 us)
Async XLA Ops:
  7.2 303.3 %copy-start = (bf16[1,512,2048]{2,1,0:T(8,128)(2,1)S(1)}, bf16[1,512,2048]{2,1,0:T(8,128)(2,1)}, u32[]{:S(2)}) copy-start(bf16[1,512,2048]{2,1,0:T(8,128)(2,1)} %param.5) | copy-start | bytes 6291460
  17.4 287.8 %all-to-all-start = ((bf16[64,128,2,384]{3,2,1,0:T(2,128)(2,1)}), bf16[64,128,2,384]{3,2,1,0:T(2,128)(2,1)}, u32[]{:S(2)}, u32[]{:S(2)}) async-start(bf16[64,128,2,384]{3,2,1,0:T(2,128)(2,1)} %stack.5), calls=%async_computation | async-start | bytes 25165824 | tf_op jit(solution)/shard_map/all_to_all | solution.py:29
  313.4 9.2 %copy-start.1 = (bf16[1,128,2,384]{3,2,1,0:T(2,128)(2,1)S(1)}, bf16[1,128,2,384]{3,2,1,0:T(2,128)(2,1)}, u32[]{:S(2)}) copy-start(bf16[1,128,2,384]{3,2,1,0:T(2,128)(2,1)} %param.6) | copy-start | bytes 589828
  313.4 9.5 %copy-start.2 = (bf16[1,2,6,384]{3,1,2,0:T(2,128)(2,1)S(1)}, bf16[1,2,6,384]{3,1,2,0:T(2,128)(2,1)}, u32[]{:S(2)}) copy-start(bf16[1,2,6,384]{3,1,2,0:T(2,128)(2,1)} %param.8) | copy-start | bytes 27652
  313.4 38.0 %all-to-all-start.1 = ((f32[4,128,768]{2,1,0:T(8,128)}), f32[4,128,768]{2,1,0:T(8,128)}, u32[]{:S(2)}, u32[]{:S(2)}) async-start(f32[4,128,768]{2,1,0:T(8,128)} %bitcast.22), calls=%async_computation.1 | async-start | bytes 3145728 | tf_op jit(solution)/shard_map/all_to_all | solution.py:15
  322.0 318.5 %all-reduce.2.cloned.1.call-start = ((), (), s32[]{:S(2)}) async-start(), calls=%async_computation.2 | async-start | bytes 2359296 | tf_op jit(solution)/shard_map/psum | solution.py:57
Sparse Core Ops, SparseCore 0:
  358.4 282.0 all-reduce.1
